TPU v7x, 256 devices: a whole 4x4x8 slice. The times are simulated.
256 devices in a mesh: expert: 32 (over y, z_lo, x), replica: 8 (over z_hi, core).
Axes of the slice: x: 4, y: 4, z: 8 (z_hi: 4, z_lo: 2; z = z_hi * 2 + z_lo), core: 2. Of those that a mesh axis runs over, the one named last changes fastest.
Arguments:
- tokens: bfloat16 [4096, 4096], P('expert', 'replica'), may hold values from -6 to 6
- out_grad: bfloat16 [4096, 4096], P('expert', 'replica'), may hold values from -6 to 6
- expert_ids: int32 [4096, 8], P('expert'), may hold values from 0 to 63, all different within a row; in each aligned block of 128 rows (0 to 127, 128 to 255, ...) at most 20 rows name the same one
- route_weight: float32 [4096, 8], P('expert'), may hold values from 0.05 to 0.3
- gate_weight: bfloat16 [64, 4096, 768], P('expert', 'replica'), may hold values from -0.09375 to 0.09375
- up_weight: bfloat16 [64, 4096, 768], P('expert', 'replica'), may hold values from -0.09375 to 0.09375
- down_weight: bfloat16 [64, 768, 4096], P('expert', None, 'replica'), may hold values from -0.21875 to 0.21875
Outputs:
- mixed: bfloat16 [4096, 4096], P('expert', 'replica')
- in_grad: bfloat16 [4096, 4096], P('expert', 'replica')
- grad_gate: bfloat16 [64, 4096, 768], P('expert', 'replica')
- grad_up: bfloat16 [64, 4096, 768], P('expert', 'replica')
- grad_down: bfloat16 [64, 768, 4096], P('expert', None, 'replica')
Inputs may be any that keep to these rules, and one draw needn't show every extreme that they name: `expert_ids`: each token names 8 different experts. Within the 128 rows of one index of expert no expert is named more than 20 times, a bound that some block reaches.
All inputs are finite; a program needn't handle non-finite values.
Results may differ from a plain program's by a relative error of at most 0.0064.
Values may be sent and summed in bfloat16 or wider, within the bound.
No kernel may reach another device: no remote copies, remote signals or barrier semaphores. Data moves between devices by JAX's collectives and lax.ppermute only.
A program may use at most 128 MiB of HBM per device.

v0:
```python
import jax
import jax.numpy as jnp
from jax import lax
from jax.sharding import PartitionSpec as P


def local(tokens, out_grad, expert_ids, route_weight, gate_weight, up_weight, down_weight):
    n_cols = lax.axis_size("expert")
    n_reps = lax.axis_size("replica")
    tok_count, topk = expert_ids.shape
    local_experts = gate_weight.shape[0]
    width = gate_weight.shape[2]
    experts_all = local_experts * n_cols
    capacity = tok_count * topk * 5 // (4 * experts_all)
    slots = experts_all * capacity
    share_rows = n_cols // n_reps
    flat_ids = expert_ids.reshape(-1)
    onehot = (flat_ids[:, None] == jnp.arange(experts_all, dtype=jnp.int32)[None, :]).astype(
        jnp.int32
    )
    ranks = jnp.sum((jnp.cumsum(onehot, axis=0) - 1) * onehot, axis=1)
    target = flat_ids * capacity + ranks
    place = (target[:, None] == jnp.arange(slots, dtype=jnp.int32)[None, :]).astype(jnp.float32)
    slot_weight = jnp.sum(place * route_weight.reshape(-1)[:, None], axis=0)
    place = place.reshape(tok_count, topk, slots)
    picker = jnp.sum(place, axis=1).astype(jnp.bfloat16)
    feats = tokens.shape[1]
    send_x = lax.dot_general(
        picker, tokens, (((0,), (0,)), ((), ())), preferred_element_type=jnp.float32
    ).astype(jnp.bfloat16)
    picked_g = lax.dot_general(
        picker, out_grad, (((0,), (0,)), ((), ())), preferred_element_type=jnp.float32
    )
    send_g = (slot_weight[:, None] * picked_g).astype(jnp.bfloat16)
    send_x = send_x.reshape(n_cols, local_experts, capacity, feats)
    send_g = send_g.reshape(n_cols, local_experts, capacity, feats)
    recv_x = lax.all_to_all(send_x, "expert", split_axis=0, concat_axis=0, tiled=True)
    replica_index = lax.axis_index("replica")
    piece = recv_x
    gate_part = jnp.einsum("jecd,edh->jech", piece, gate_weight, preferred_element_type=jnp.float32)
    up_part = jnp.einsum("jecd,edh->jech", piece, up_weight, preferred_element_type=jnp.float32)
    summed = lax.psum(jnp.concatenate([gate_part, up_part], axis=3), "replica")
    gate_all = summed[..., :width]
    hidden = (jax.nn.silu(gate_all) * summed[..., width:]).astype(jnp.bfloat16)
    share = lax.dynamic_slice_in_dim(summed, replica_index * share_rows, share_rows, 0)
    gate_share = share[..., :width]
    up_share = share[..., width:]
    expert_out = jnp.einsum(
        "jech,ehd->jecd", hidden, down_weight, preferred_element_type=jnp.float32
    ).astype(jnp.bfloat16)
    returned = lax.all_to_all(expert_out, "expert", split_axis=0, concat_axis=0, tiled=True)
    chosen_rows = jnp.take(returned.reshape(slots, feats), target, axis=0).astype(jnp.float32)
    chosen_rows = chosen_rows.reshape(tok_count, topk, feats)
    mixed = jnp.sum(route_weight[:, :, None] * chosen_rows, axis=1).astype(jnp.bfloat16)
    recv_g = lax.all_to_all(send_g, "expert", split_axis=0, concat_axis=0, tiled=True)
    grad_down = jnp.einsum(
        "jech,jecd->ehd", hidden, recv_g, preferred_element_type=jnp.float32
    ).astype(jnp.bfloat16)
    piece = recv_g
    hidden_grad = lax.psum_scatter(
        jnp.einsum("jecd,ehd->jech", piece, down_weight, preferred_element_type=jnp.float32),
        "replica",
        scatter_dimension=0,
        tiled=True,
    )
    sig = jax.nn.sigmoid(gate_share)
    act = gate_share * sig
    gate_grad = (hidden_grad * up_share * sig * (1.0 + gate_share * (1.0 - sig))).astype(
        jnp.bfloat16
    )
    up_grad = (hidden_grad * act).astype(jnp.bfloat16)
    both_grads = lax.all_gather(
        jnp.concatenate([gate_grad, up_grad], axis=3), "replica", axis=0, tiled=True
    )
    gate_all_grad = both_grads[..., :width]
    up_all_grad = both_grads[..., width:]
    grad_gate = jnp.einsum(
        "jecd,jech->edh", recv_x, gate_all_grad, preferred_element_type=jnp.float32
    ).astype(jnp.bfloat16)
    grad_up = jnp.einsum(
        "jecd,jech->edh", recv_x, up_all_grad, preferred_element_type=jnp.float32
    ).astype(jnp.bfloat16)
    slot_in = (
        jnp.einsum("jech,edh->jecd", gate_all_grad, gate_weight, preferred_element_type=jnp.float32)
        + jnp.einsum("jech,edh->jecd", up_all_grad, up_weight, preferred_element_type=jnp.float32)
    ).astype(jnp.bfloat16)
    back_in = lax.all_to_all(slot_in, "expert", split_axis=0, concat_axis=0, tiled=True)
    in_grad = jnp.dot(
        picker, back_in.reshape(slots, feats), preferred_element_type=jnp.float32
    ).astype(jnp.bfloat16)
    return (mixed, in_grad, grad_gate, grad_up, grad_down)


def solution(mesh):
    in_specs = (
        P("expert", "replica"),
        P("expert", "replica"),
        P("expert", None),
        P("expert", None),
        P("expert", "replica", None),
        P("expert", "replica", None),
        P("expert", None, "replica"),
    )
    out_specs = (
        P("expert", "replica"),
        P("expert", "replica"),
        P("expert", "replica", None),
        P("expert", "replica", None),
        P("expert", None, "replica"),
    )
    return jax.shard_map(local, mesh=mesh, in_specs=in_specs, out_specs=out_specs, check_vma=False)
```

profile of v0, /device:TPU:1, one launch (start us, length us, event | category | flops | bytes accessed | tf_op | source)
XLA Modules:
  0.0 471.5 jit_solution(4206737577058164144)
XLA Ops:
  8.3 18.0 %reduce-window.6 = s32[64,8,128]{2,1,0:T(8,128)S(1)} reduce-window(s32[64,8,128]{2,1,0:T(8,128)S(1)} %fusion.37, s32[]{:T(128)} %constant.16.clone.1), window={size=1x1x128 pad=0_0x0_0x127_0}, to_apply=%region_0.0 | reduce-window | flops 8323072 | bytes 524292 | tf_op jit(solution)/shard_map/reduce-window
  27.2 1.6 convert_reduce_fusion
  30.7 3.5 copy.100
  34.2 9.3 %all-to-all-start = ((bf16[32,2,20,512]{3,1,2,0:T(2,128)(2,1)}), bf16[32,2,20,512]{3,1,2,0:T(2,128)(2,1)S(1)}, u32[]{:S(2)}, u32[]{:S(2)}) async-start(bf16[32,2,20,512]{3,1,2,0:T(2,128)(2,1)} %copy.100), calls=%async_computation | async-start | bytes 2621440 | tf_op jit(solution)/shard_map/all_to_all | solution.py:37
  44.4 1.6 fusion.1
  46.0 3.2 reshape.108
  49.2 3.5 copy.107
  52.7 9.0 %all-to-all-done = bf16[32,2,20,512]{3,1,2,0:T(2,128)(2,1)S(1)} async-done(((bf16[32,2,20,512]{3,1,2,0:T(2,128)(2,1)}), bf16[32,2,20,512]{3,1,2,0:T(2,128)(2,1)S(1)}, u32[]{:S(2)}, u32[]{:S(2)}) %all-to-all-start) | async-done | bytes 1310752 | tf_op jit(solution)/shard_map/all_to_all | solution.py:37
  61.7 6.4 %all-to-all-start.2 = ((bf16[32,2,20,512]{3,1,2,0:T(2,128)(2,1)}), bf16[32,2,20,512]{3,1,2,0:T(2,128)(2,1)}, u32[]{:S(2)}, u32[]{:S(2)}) async-start(bf16[32,2,20,512]{3,1,2,0:T(2,128)(2,1)} %copy.107), calls=%async_computation.2 | async-start | bytes 2621440 | tf_op jit(solution)/shard_map/all_to_all | solution.py:55
  68.3 2.9 convolution_bitcast_fusion.1
  71.2 1.4 convolution_bitcast_fusion.2
  72.7 4.1 pad_maximum_fusion
  76.8 8.8 %all-to-all-done.2 = bf16[32,2,20,512]{3,1,2,0:T(2,128)(2,1)} async-done(((bf16[32,2,20,512]{3,1,2,0:T(2,128)(2,1)}), bf16[32,2,20,512]{3,1,2,0:T(2,128)(2,1)}, u32[]{:S(2)}, u32[]{:S(2)}) %all-to-all-start.2) | async-done | bytes 1310752 | tf_op jit(solution)/shard_map/all_to_all | solution.py:55
  85.6 4.7 convolution_bitcast_fusion
  92.2 254.9 %all-reduce.4.cloned.1.call-done = (f32[32,2,20,1536]{3,0,2,1:T(8,128)}, f32[32,2,20,768]{3,0,2,1:T(8,128)}) async-done(((f32[32,2,20,1536]{3,0,2,1:T(8,128)}, f32[32,2,20,768]{3,0,2,1:T(8,128)}), (f32[32,2,20,1536]{3,0,2,1:T(8,128)}, f32[32,2,20,768]{3,0,2,1:T(8,128)})) %all-reduce.4.cloned.1.call-update) | async-done | bytes 11796496 | tf_op jit(solution)/shard_map/psum | solution.py:42
  347.1 2.5 fusion.34
  351.1 4.5 fusion
  356.9 2.4 copy.103
  359.3 8.5 %all-to-all-start.1 = ((bf16[32,2,20,512]{3,1,2,0:T(2,128)(2,1)}), bf16[32,2,20,512]{3,1,2,0:T(2,128)(2,1)}, u32[]{:S(2)}, u32[]{:S(2)}) async-start(bf16[32,2,20,512]{3,1,2,0:T(2,128)(2,1)} %copy.103), calls=%async_computation.1 | async-start | bytes 2621440 | tf_op jit(solution)/shard_map/all_to_all | solution.py:51
  368.2 46.5 %all-gather.2.cloned.1.call-done = bf16[32,2,20,1536]{3,1,2,0:T(2,128)(2,1)} async-done(((bf16[4,2,20,1536]{3,1,2,0:T(2,128)(2,1)}), bf16[32,2,20,1536]{3,1,2,0:T(2,128)(2,1)}) %all-gather.2.cloned.1.call-update) | async-done | bytes 3932176 | tf_op jit(solution)/shard_map/all_gather | solution.py:72
  414.7 4.6 fusion.43
  423.2 2.5 copy.112
  425.7 7.0 %all-to-all-start.3 = ((bf16[32,2,20,512]{3,1,2,0:T(2,128)(2,1)}), bf16[32,2,20,512]{3,1,2,0:T(2,128)(2,1)}, u32[]{:S(2)}, u32[]{:S(2)}) async-start(bf16[32,2,20,512]{3,1,2,0:T(2,128)(2,1)} %copy.112), calls=%async_computation.3 | async-start | bytes 2621440 | tf_op jit(solution)/shard_map/all_to_all | solution.py:87
  432.6 4.6 bitcast_convert_fusion
  437.2 2.8 copy.104
  440.0 2.3 reshape.107
  442.3 5.1 %gather_fusion = bf16[1024,512]{1,0:T(8,128)(2,1)} fusion(bf16[1280,512]{1,0:T(8,128)(2,1)S(1)} %reshape.107, s32[1024]{0:T(1024)S(1)} %broadcast_clamp_fusion), kind=kCustom, calls=%fused_computation | custom fusion | bytes 2101248 | tf_op jit(solution)/shard_map/jit(_take)/gather | solution.py:52
  447.4 2.7 multiply_reduce_fusion
  450.0 5.0 %bitcast_convert_fusion.1 = bf16[2,512,768]{2,1,0:T(8,128)(2,1)} fusion(bf16[32,2,20,768]{3,1,2,0:T(2,128)(2,1)} %copy-done.7, bf16[32,2,20,512]{3,1,2,0:T(2,128)(2,1)S(1)} %all-to-all-done), kind=kOutput, calls=%fused_computation.10 | convolution fusion | flops 1007419392 | bytes 4849664 | tf_op jit(solution)/shard_map/jecd,jech->edh/dot_general | solution.py:80
  455.0 3.3 bitcast_convert_fusion.2
  458.4 2.9 copy.113
  461.3 2.3 reshape.109
  (68 shorter events, 14.1 us)
Async XLA Ops:
  7.2 78.4 %copy-start = (bf16[2,768,512]{2,1,0:T(8,128)(2,1)S(1)}, bf16[2,768,512]{2,1,0:T(8,128)(2,1)}, u32[]{:S(2)}) copy-start(bf16[2,768,512]{2,1,0:T(8,128)(2,1)} %param.13) | copy-start | bytes 4718596
  7.2 19.9 %copy-start.11 = (s32[128,8]{0,1:T(8,128)S(1)}, s32[128,8]{0,1:T(8,128)}, u32[]{:S(2)}) copy-start(s32[128,8]{0,1:T(8,128)} %param.9) | copy-start | bytes 12292
  7.2 21.7 %copy-start.9 = (bf16[128,512]{1,0:T(8,128)(2,1)S(1)}, bf16[128,512]{1,0:T(8,128)(2,1)}, u32[]{:S(2)}) copy-start(bf16[128,512]{1,0:T(8,128)(2,1)} %param.7) | copy-start | bytes 393220
  34.1 9.4 %copy-start.12 = (f32[128,8]{0,1:T(8,128)S(1)}, f32[128,8]{0,1:T(8,128)}, u32[]{:S(2)}) copy-start(f32[128,8]{0,1:T(8,128)} %param.10) | copy-start | bytes 12292
  34.1 10.2 %copy-start.10 = (bf16[128,512]{1,0:T(8,128)(2,1)S(1)}, bf16[128,512]{1,0:T(8,128)(2,1)}, u32[]{:S(2)}) copy-start(bf16[128,512]{1,0:T(8,128)(2,1)} %param.8) | copy-start | bytes 393220
  34.2 27.5 %all-to-all-start = ((bf16[32,2,20,512]{3,1,2,0:T(2,128)(2,1)}), bf16[32,2,20,512]{3,1,2,0:T(2,128)(2,1)S(1)}, u32[]{:S(2)}, u32[]{:S(2)}) async-start(bf16[32,2,20,512]{3,1,2,0:T(2,128)(2,1)} %copy.100), calls=%async_computation | async-start | bytes 2621440 | tf_op jit(solution)/shard_map/all_to_all | solution.py:37
  61.7 23.9 %all-to-all-start.2 = ((bf16[32,2,20,512]{3,1,2,0:T(2,128)(2,1)}), bf16[32,2,20,512]{3,1,2,0:T(2,128)(2,1)}, u32[]{:S(2)}, u32[]{:S(2)}) async-start(bf16[32,2,20,512]{3,1,2,0:T(2,128)(2,1)} %copy.107), calls=%async_computation.2 | async-start | bytes 2621440 | tf_op jit(solution)/shard_map/all_to_all | solution.py:55
  68.1 279.0 %all-reduce.4.cloned.1.call-start = ((), (), s32[]{:S(2)}) async-start(), calls=%async_computation.5 | async-start | bytes 23592960 | tf_op jit(solution)/shard_map/psum | solution.py:42
  68.3 2.9 copy-start.4
  90.3 0.7 copy-start.13
  90.3 324.4 %all-gather.2.cloned.1.call-start = ((), (), s32[]{:S(2)}) async-start(), calls=%async_computation.4 | async-start | bytes 4423680 | tf_op jit(solution)/shard_map/all_gather | solution.py:72
  355.6 1.3 copy-start.6
  359.3 66.4 %all-to-all-start.1 = ((bf16[32,2,20,512]{3,1,2,0:T(2,128)(2,1)}), bf16[32,2,20,512]{3,1,2,0:T(2,128)(2,1)}, u32[]{:S(2)}, u32[]{:S(2)}) async-start(bf16[32,2,20,512]{3,1,2,0:T(2,128)(2,1)} %copy.103), calls=%async_computation.1 | async-start | bytes 2621440 | tf_op jit(solution)/shard_map/all_to_all | solution.py:51
  414.7 4.6 copy-start.8
  419.3 1.3 copy-start.7
  419.3 1.9 copy-start.2
  419.3 2.6 copy-start.5
  425.7 32.7 %all-to-all-start.3 = ((bf16[32,2,20,512]{3,1,2,0:T(2,128)(2,1)}), bf16[32,2,20,512]{3,1,2,0:T(2,128)(2,1)}, u32[]{:S(2)}, u32[]{:S(2)}) async-start(bf16[32,2,20,512]{3,1,2,0:T(2,128)(2,1)} %copy.112), calls=%async_computation.3 | async-start | bytes 2621440 | tf_op jit(solution)/shard_map/all_to_all | solution.py:87
  450.0 5.0 %copy-start.3 = (bf16[32,2,20,768]{3,1,2,0:T(2,128)(2,1)S(1)}, bf16[32,2,20,768]{3,1,2,0:T(2,128)(2,1)}, u32[]{:S(2)}) copy-start(bf16[32,2,20,768]{3,1,2,0:T(2,128)(2,1)} %copy-done.2) | copy-start | bytes 5898244
  458.4 6.2 %copy-start.1 = (bf16[2,768,512]{2,1,0:T(8,128)(2,1)S(1)}, bf16[2,768,512]{2,1,0:T(8,128)(2,1)}, u32[]{:S(2)}) copy-start(bf16[2,768,512]{2,1,0:T(8,128)(2,1)} %param.13) | copy-start | bytes 4718596
Sparse Core Ops, SparseCore 0:
  90.4 256.6 all-reduce.3
  351.2 63.4 all-gather.1
where the time goes:
time: 472 us; the launch traced here: 471 us
  waiting for transfers between devices  319 us (68%)
  local copies, waits for them, and re-layouts  42.4 us (9%)
  other arithmetic  34.6 us (7%)
  starting transfers between devices  31.5 us (7%)
  matrix products  28.7 us (6%)
  between operations  15 us (3%)
    psum x1, waiting for transfers between devices, local(): summed = lax.psum(jnp.concatenate([gate_part, up_part], axis=3), 'replica')  255 us
    all_gather x1, waiting for transfers between devices, local(): lax.all_gather(jnp.concatenate([gate_grad, up_grad], axis=3), 'replica',...  46.5 us
    another operation x2, other arithmetic  18 us
  transfers between devices with their start and end apart: 6, of which 4 were waited for; matrix products, arithmetic and copies ran while one was open for 13% of the time, Pallas kernels for 0%

commit v1 on v0

--- a/solution.py
+++ b/solution.py
@@ -69,8 +69,14 @@
         jnp.bfloat16
     )
     up_grad = (hidden_grad * act).astype(jnp.bfloat16)
-    both_grads = lax.all_gather(
-        jnp.concatenate([gate_grad, up_grad], axis=3), "replica", axis=0, tiled=True
+    both_grads = jnp.concatenate(
+        lax.all_to_all(
+            jnp.stack([jnp.concatenate([gate_grad, up_grad], axis=3)] * lax.axis_size("replica")),
+            "replica",
+            0,
+            0,
+        ),
+        axis=0,
     )
     gate_all_grad = both_grads[..., :width]
     up_all_grad = both_grads[..., width:]

time: 472 us -> 524 us (1.11)
  starting transfers between devices: 31.5 us -> 51.9 us
  waiting for transfers between devices: 319 us -> 336 us
  local copies, waits for them, and re-layouts: 42.4 us -> 52.1 us
    all_to_all x0 -> x1, waiting for transfers between devices: none -> 63.5 us  [local(): lax.all_to_all(jnp.stack([jnp.concatenate([gate_grad, up_grad], axis=3)]...]
    all_gather x1 -> x0, waiting for transfers between devices: 46.5 us -> none  [local(): lax.all_gather(jnp.concatenate([gate_grad, up_grad], axis=3), 'replica',...]
    all_to_all x1, starting transfers between devices: 8.53 us -> 23.5 us  [local(): lax.all_to_all(expert_out, 'expert', split_axis=0, concat_axis=0, tiled=T...]
    reshape x0 -> x1, local copies, waits for them, and re-layouts: none -> 7.12 us  [local(): jnp.concatenate(lax.all_to_all(jnp.stack([jnp.concatenate([gate_grad, up_...]
    all_to_all x0 -> x1, local copies, waits for them, and re-layouts: none -> 6.08 us  [local(): lax.all_to_all(jnp.stack([jnp.concatenate([gate_grad, up_grad], axis=3)]...]
  transfers between devices with their start and end apart: 6 -> 6, of which waited for: 4 -> 4; matrix products, arithmetic and copies ran while one was open for 13% -> 14% of each run, Pallas kernels for 0% -> 0%
where the time goes in v1:
time: 524 us; the launch traced here: 520 us
  waiting for transfers between devices  336 us (64%)
  local copies, waits for them, and re-layouts  52.1 us (10%)
  starting transfers between devices  51.9 us (10%)
  other arithmetic  34.6 us (7%)
  matrix products  30.3 us (6%)
  between operations  15 us (3%)
    psum x1, waiting for transfers between devices, local(): summed = lax.psum(jnp.concatenate([gate_part, up_part], axis=3), 'replica')  255 us
    all_to_all x1, waiting for transfers between devices, local(): lax.all_to_all(jnp.stack([jnp.concatenate([gate_grad, up_grad], axis=3)]...  63.5 us
    all_to_all x1, starting transfers between devices, local(): lax.all_to_all(expert_out, 'expert', split_axis=0, concat_axis=0, tiled=T...  23.5 us
    another operation x2, other arithmetic  18 us
  transfers between devices with their start and end apart: 6, of which 4 were waited for; matrix products, arithmetic and copies ran while one was open for 14% of the time, Pallas kernels for 0%

profile of v1, /device:TPU:1, one launch (start us, length us, event | category | flops | bytes accessed | tf_op | source)
XLA Modules:
  0.0 520.2 jit_solution(5123877012896466721)
XLA Ops:
  8.3 18.0 %reduce-window.6 = s32[64,8,128]{2,1,0:T(8,128)S(1)} reduce-window(s32[64,8,128]{2,1,0:T(8,128)S(1)} %fusion.37, s32[]{:T(128)} %constant.16.clone.1), window={size=1x1x128 pad=0_0x0_0x127_0}, to_apply=%region_0.0 | reduce-window | flops 8323072 | bytes 524292 | tf_op jit(solution)/shard_map/reduce-window
  30.7 3.5 copy.94
  34.2 9.3 %all-to-all-start = ((bf16[32,2,20,512]{3,1,2,0:T(2,128)(2,1)}), bf16[32,2,20,512]{3,1,2,0:T(2,128)(2,1)S(1)}, u32[]{:S(2)}, u32[]{:S(2)}) async-start(bf16[32,2,20,512]{3,1,2,0:T(2,128)(2,1)} %copy.94), calls=%async_computation | async-start | bytes 2621440 | tf_op jit(solution)/shard_map/all_to_all | solution.py:37
  46.0 3.2 reshape.113
  49.2 3.5 copy.101
  52.7 9.0 %all-to-all-done = bf16[32,2,20,512]{3,1,2,0:T(2,128)(2,1)S(1)} async-done(((bf16[32,2,20,512]{3,1,2,0:T(2,128)(2,1)}), bf16[32,2,20,512]{3,1,2,0:T(2,128)(2,1)S(1)}, u32[]{:S(2)}, u32[]{:S(2)}) %all-to-all-start) | async-done | bytes 1310752 | tf_op jit(solution)/shard_map/all_to_all | solution.py:37
  61.7 6.4 %all-to-all-start.2 = ((bf16[32,2,20,512]{3,1,2,0:T(2,128)(2,1)}), bf16[32,2,20,512]{3,1,2,0:T(2,128)(2,1)}, u32[]{:S(2)}, u32[]{:S(2)}) async-start(bf16[32,2,20,512]{3,1,2,0:T(2,128)(2,1)} %copy.101), calls=%async_computation.2 | async-start | bytes 2621440 | tf_op jit(solution)/shard_map/all_to_all | solution.py:55
  68.3 2.9 convolution_bitcast_fusion.1
  72.7 4.1 pad_maximum_fusion
  76.8 8.8 %all-to-all-done.2 = bf16[32,2,20,512]{3,1,2,0:T(2,128)(2,1)} async-done(((bf16[32,2,20,512]{3,1,2,0:T(2,128)(2,1)}), bf16[32,2,20,512]{3,1,2,0:T(2,128)(2,1)}, u32[]{:S(2)}, u32[]{:S(2)}) %all-to-all-start.2) | async-done | bytes 1310752 | tf_op jit(solution)/shard_map/all_to_all | solution.py:55
  85.6 4.7 convolution_bitcast_fusion
  92.2 254.9 %all-reduce.4.cloned.1.call-done = (f32[32,2,20,1536]{3,0,2,1:T(8,128)}, f32[32,2,20,768]{3,0,2,1:T(8,128)}) async-done(((f32[32,2,20,1536]{3,0,2,1:T(8,128)}, f32[32,2,20,768]{3,0,2,1:T(8,128)}), (f32[32,2,20,1536]{3,0,2,1:T(8,128)}, f32[32,2,20,768]{3,0,2,1:T(8,128)})) %all-reduce.4.cloned.1.call-update) | async-done | bytes 11796496 | tf_op jit(solution)/shard_map/psum | solution.py:42
  347.1 2.5 fusion.34
  349.8 3.5 stack.2
  353.3 4.9 all-to-all-start.3
  358.2 4.5 fusion
  364.0 2.4 copy.97
  366.4 63.5 %all-to-all-done.3 = bf16[8,4,2,20,1536]{4,1,3,2,0:T(4,128)(2,1)} async-done(((bf16[8,4,2,20,1536]{4,1,3,2,0:T(4,128)(2,1)}), bf16[8,4,2,20,1536]{4,1,3,2,0:T(4,128)(2,1)}, u32[]{:S(2)}, u32[]{:S(2)}) %all-to-all-start.3) | async-done | bytes 3932192 | tf_op jit(solution)/shard_map/all_to_all | solution.py:73
  429.9 23.5 %all-to-all-start.1 = ((bf16[32,2,20,512]{3,1,2,0:T(2,128)(2,1)}), bf16[32,2,20,512]{3,1,2,0:T(2,128)(2,1)}, u32[]{:S(2)}, u32[]{:S(2)}) async-start(bf16[32,2,20,512]{3,1,2,0:T(2,128)(2,1)} %copy.97), calls=%async_computation.1 | async-start | bytes 2621440 | tf_op jit(solution)/shard_map/all_to_all | solution.py:51
  453.8 6.1 %copy.103 = bf16[8,4,2,20,1536]{4,1,0,3,2:T(4,128)(2,1)} copy(bf16[8,4,2,20,1536]{4,1,3,2,0:T(4,128)(2,1)} %all-to-all-done.3) | data formatting | bytes 7864320 | tf_op jit(solution)/shard_map/all_to_all | solution.py:73
  459.9 7.1 %reshape.114 = bf16[32,2,20,1536]{3,0,2,1:T(8,128)(2,1)} reshape(bf16[8,4,2,20,1536]{4,1,0,3,2:T(4,128)(2,1)} %copy.103) | data formatting | bytes 7864320 | tf_op jit(solution)/shard_map/reshape | solution.py:72
  467.0 3.4 fusion.3
  471.9 2.4 copy.104
  474.3 7.6 %all-to-all-start.4 = ((bf16[32,2,20,512]{3,1,2,0:T(2,128)(2,1)}), bf16[32,2,20,512]{3,1,2,0:T(2,128)(2,1)}, u32[]{:S(2)}, u32[]{:S(2)}) async-start(bf16[32,2,20,512]{3,1,2,0:T(2,128)(2,1)} %copy.104), calls=%async_computation.4 | async-start | bytes 2621440 | tf_op jit(solution)/shard_map/all_to_all | solution.py:93
  481.9 4.6 bitcast_convert_fusion
  486.5 2.8 copy.98
  491.5 5.1 gather_fusion
  496.6 2.7 multiply_reduce_fusion
  499.3 4.7 bitcast_convert_fusion.1
  504.0 3.1 bitcast_convert_fusion.2
  507.2 2.8 copy.105
  510.0 2.4 reshape.115
  (64 shorter events, 17.4 us)
Async XLA Ops:
  7.2 78.4 %copy-start = (bf16[2,768,512]{2,1,0:T(8,128)(2,1)S(1)}, bf16[2,768,512]{2,1,0:T(8,128)(2,1)}, u32[]{:S(2)}) copy-start(bf16[2,768,512]{2,1,0:T(8,128)(2,1)} %param.13) | copy-start | bytes 4718596
  7.2 19.9 %copy-start.9 = (s32[128,8]{0,1:T(8,128)S(1)}, s32[128,8]{0,1:T(8,128)}, u32[]{:S(2)}) copy-start(s32[128,8]{0,1:T(8,128)} %param.9) | copy-start | bytes 12292
  8.2 20.7 %copy-start.7 = (bf16[128,512]{1,0:T(8,128)(2,1)S(1)}, bf16[128,512]{1,0:T(8,128)(2,1)}, u32[]{:S(2)}) copy-start(bf16[128,512]{1,0:T(8,128)(2,1)} %param.7) | copy-start | bytes 393220
  34.1 9.4 %copy-start.10 = (f32[128,8]{0,1:T(8,128)S(1)}, f32[128,8]{0,1:T(8,128)}, u32[]{:S(2)}) copy-start(f32[128,8]{0,1:T(8,128)} %param.10) | copy-start | bytes 12292
  34.1 10.2 %copy-start.8 = (bf16[128,512]{1,0:T(8,128)(2,1)S(1)}, bf16[128,512]{1,0:T(8,128)(2,1)}, u32[]{:S(2)}) copy-start(bf16[128,512]{1,0:T(8,128)(2,1)} %param.8) | copy-start | bytes 393220
  34.2 27.5 %all-to-all-start = ((bf16[32,2,20,512]{3,1,2,0:T(2,128)(2,1)}), bf16[32,2,20,512]{3,1,2,0:T(2,128)(2,1)S(1)}, u32[]{:S(2)}, u32[]{:S(2)}) async-start(bf16[32,2,20,512]{3,1,2,0:T(2,128)(2,1)} %copy.94), calls=%async_computation | async-start | bytes 2621440 | tf_op jit(solution)/shard_map/all_to_all | solution.py:37
  61.7 23.9 %all-to-all-start.2 = ((bf16[32,2,20,512]{3,1,2,0:T(2,128)(2,1)}), bf16[32,2,20,512]{3,1,2,0:T(2,128)(2,1)}, u32[]{:S(2)}, u32[]{:S(2)}) async-start(bf16[32,2,20,512]{3,1,2,0:T(2,128)(2,1)} %copy.101), calls=%async_computation.2 | async-start | bytes 2621440 | tf_op jit(solution)/shard_map/all_to_all | solution.py:55
  68.1 279.0 %all-reduce.4.cloned.1.call-start = ((), (), s32[]{:S(2)}) async-start(), calls=%async_computation.5 | async-start | bytes 23592960 | tf_op jit(solution)/shard_map/psum | solution.py:42
  68.3 2.9 copy-start.4
  90.3 0.7 copy-start.11
  353.3 76.7 %all-to-all-start.3 = ((bf16[8,4,2,20,1536]{4,1,3,2,0:T(4,128)(2,1)}), bf16[8,4,2,20,1536]{4,1,3,2,0:T(4,128)(2,1)}, u32[]{:S(2)}, u32[]{:S(2)}) async-start(bf16[8,4,2,20,1536]{4,1,3,2,0:T(4,128)(2,1)} %stack.2), calls=%async_computation.3 | async-start | bytes 7864320 | tf_op jit(solution)/shard_map/all_to_all | solution.py:73
  362.7 1.3 copy-start.6
  429.9 44.4 %all-to-all-start.1 = ((bf16[32,2,20,512]{3,1,2,0:T(2,128)(2,1)}), bf16[32,2,20,512]{3,1,2,0:T(2,128)(2,1)}, u32[]{:S(2)}, u32[]{:S(2)}) async-start(bf16[32,2,20,512]{3,1,2,0:T(2,128)(2,1)} %copy.97), calls=%async_computation.1 | async-start | bytes 2621440 | tf_op jit(solution)/shard_map/all_to_all | solution.py:51
  467.0 3.4 copy-start.2
  467.0 3.7 copy-start.5
  474.3 32.9 %all-to-all-start.4 = ((bf16[32,2,20,512]{3,1,2,0:T(2,128)(2,1)}), bf16[32,2,20,512]{3,1,2,0:T(2,128)(2,1)}, u32[]{:S(2)}, u32[]{:S(2)}) async-start(bf16[32,2,20,512]{3,1,2,0:T(2,128)(2,1)} %copy.104), calls=%async_computation.4 | async-start | bytes 2621440 | tf_op jit(solution)/shard_map/all_to_all | solution.py:93
  499.3 4.7 copy-start.3
  510.0 3.4 copy-start.1
Sparse Core Ops, SparseCore 0:
  90.4 256.6 all-reduce.3
